TPU v7x, 256 devices: a whole 4x4x8 slice. The times are simulated.
256 devices in a mesh: enc: 8 (over z), kr: 8 (over x_lo, y), kc: 4 (over x_hi, core).
Axes of the slice: x: 4 (x_hi: 2, x_lo: 2; x = x_hi * 2 + x_lo), y: 4, z: 8, core: 2. Of those that a mesh axis runs over, the one named last changes fastest.
Arguments:
- inputs: bfloat16 [49152, 1024], P(('enc', 'kr', 'kc')), may hold values from -24 to 24
- w_first: bfloat16 [1024, 1024], replicated, may hold values from -0.1875 to 0.1875
- w_second: bfloat16 [1024, 64], replicated, may hold values from -0.1875 to 0.1875
- inv_length: float32 [64], replicated, may hold values from 0.05 to 1.8
- probes: bfloat16 [49152, 128], P(('enc', 'kr', 'kc')), may hold values from -6 to 6
- solves: bfloat16 [49152, 128], P(('enc', 'kr', 'kc')), may hold values from -6 to 6
Outputs:
- products: bfloat16 [49152, 128], P(('enc', 'kr', 'kc'))
- grad_first: float32 [1024, 1024], P(('enc', 'kr', 'kc'))
- grad_second: float32 [1024, 64], P(('enc', 'kr', 'kc'))
All inputs are finite; a program needn't handle non-finite values.
Results may differ from a plain program's by a relative error of at most 0.007.
The roundings to bfloat16 on the way count: a program that leaves them out, or rounds other values in their place, can miss the bound.
Values may be sent and summed in bfloat16 or wider, within the bound.
A program may use at most 64 MiB of HBM per device.

v0:
```python
import math

import jax
import jax.numpy as jnp
from jax import lax
from jax.sharding import PartitionSpec as P

probe_gain = 0.5
loss_gain = 0.02


def contract_inner(left, right):
    return lax.dot_general(
        left, right, (((1,), (1,)), ((), ())), preferred_element_type=jnp.float32
    )


def contract_outer(left, right):
    return lax.dot_general(
        left, right, (((0,), (0,)), ((), ())), preferred_element_type=jnp.float32
    )


def kernel_tile(row_feat, row_norm, col_feat):
    col_wide = col_feat.astype(jnp.float32)
    col_norm = jnp.sum(col_wide * col_wide, axis=1)
    cross = contract_inner(row_feat, col_feat)
    return jnp.exp(-0.5 * (row_norm[:, None] + col_norm[None, :] - 2.0 * cross))


def split_blocks(array):
    length = array.shape[0]
    candidates = [
        option_width
        for option_width in (1024, 768, 512, 384, 256, 192, 128)
        if length % option_width == 0
    ]
    width = candidates[0]
    return array.reshape(length // width, width, array.shape[1])


def row_totals(parts):
    return (
        lax.psum_scatter(parts[0], "kc", scatter_dimension=0, tiled=True),
        lax.psum_scatter(parts[1], "kc", scatter_dimension=0, tiled=True),
        lax.psum_scatter(parts[2], "kc", scatter_dimension=0, tiled=True),
    )


def local(inputs, w_first, w_second, inv_length, probes, solves):
    pre = jnp.dot(inputs, w_first, preferred_element_type=jnp.float32)
    hidden = jax.nn.silu(pre).astype(jnp.bfloat16)
    features = jnp.dot(hidden, w_second, preferred_element_type=jnp.float32)
    scaled = (features * inv_length[None, :]).astype(jnp.bfloat16)
    own_wide = scaled.astype(jnp.float32)
    own_rows = inputs.shape[0]
    row_count = own_rows * lax.axis_size("kc")
    feat_width = scaled.shape[1]
    probe_width = probes.shape[1]
    zeros_init = (
        jnp.zeros((row_count, probe_width), jnp.float32),
        jnp.zeros((row_count, feat_width), jnp.float32),
        jnp.zeros((row_count,), jnp.float32),
    )
    row_feat, row_probe, row_solve = (
        lax.all_gather(scaled, "kc", axis=0, tiled=True),
        lax.all_gather(probes, "kc", axis=0, tiled=True),
        lax.all_gather(solves, "kc", axis=0, tiled=True),
    )
    row_wide = row_feat.astype(jnp.float32)
    row_norm = jnp.sum(row_wide * row_wide, axis=1)
    portion = (
        lax.all_gather(scaled, ("enc", "kr"), axis=0, tiled=True),
        lax.all_gather(probes, ("enc", "kr"), axis=0, tiled=True),
        lax.all_gather(solves, ("enc", "kr"), axis=0, tiled=True),
    )

    def advance(totals, columns):
        col_feat, col_probe, col_solve = columns
        kernel = kernel_tile(row_feat, row_norm, col_feat)
        first = kernel * contract_inner(row_solve, col_probe)
        second = kernel * contract_inner(row_probe, col_solve)
        mixed_part = jnp.dot(
            first.astype(jnp.bfloat16), col_feat, preferred_element_type=jnp.float32
        ) + jnp.dot(second.astype(jnp.bfloat16), col_feat, preferred_element_type=jnp.float32)
        vpart = jnp.dot(kernel.astype(jnp.bfloat16), col_probe, preferred_element_type=jnp.float32)
        return (
            (
                totals[0] + vpart,
                totals[1] + mixed_part,
                totals[2] + jnp.sum(first, axis=1) + jnp.sum(second, axis=1),
            ),
            None,
        )

    stacked = tuple((split_blocks(item) for item in portion))
    result, _ = lax.scan(advance, zeros_init, stacked)
    vsum, mixed, sums = row_totals(result)
    products = (vsum * probe_gain).astype(jnp.bfloat16)
    lscale = loss_gain / math.sqrt(probe_width)
    dfeat = -lscale * inv_length[None, :] * (sums[:, None] * own_wide - mixed)
    dfeat_half = dfeat.astype(jnp.bfloat16)
    second_term = contract_outer(hidden, dfeat_half)
    back_hidden = contract_inner(dfeat_half, w_second)
    sigma = jax.nn.sigmoid(pre)
    dpre = (back_hidden * sigma * (1.0 + pre * (1.0 - sigma))).astype(jnp.bfloat16)
    first_term = contract_outer(inputs, dpre)
    grad_first, grad_second = (
        lax.psum_scatter(first_term, ("enc", "kr", "kc"), scatter_dimension=0, tiled=True),
        lax.psum_scatter(second_term, ("enc", "kr", "kc"), scatter_dimension=0, tiled=True),
    )
    return (products, grad_first, grad_second)


def solution(mesh):
    in_specs = (
        P(("enc", "kr", "kc"), None),
        P(),
        P(),
        P(),
        P(("enc", "kr", "kc"), None),
        P(("enc", "kr", "kc"), None),
    )
    out_specs = (
        P(("enc", "kr", "kc"), None),
        P(("enc", "kr", "kc"), None),
        P(("enc", "kr", "kc"), None),
    )
    return jax.shard_map(local, mesh=mesh, in_specs=in_specs, out_specs=out_specs, check_vma=False)
```

profile of v0, /device:TPU:1, one launch (start us, length us, event | category | flops | bytes accessed | tf_op | source)
XLA Modules:
  0.0 1430.6 jit_solution(13192146417634224073)
XLA Ops:
  8.8 2.5 multiply_convert_fusion
  13.8 10.2 all-gather
  25.6 7.3 all_gather.21
  32.9 7.1 all_gather.23
  40.9 227.9 %all-gather.10.cloned.1.call-done = bf16[64,192,64]{1,2,0:T(8,128)(2,1)} async-done(((bf16[1,192,64]{1,2,0:T(8,128)(2,1)}), bf16[64,192,64]{1,2,0:T(8,128)(2,1)}) %all-gather.10.cloned.1.call-update) | async-done | bytes 1572880 | tf_op jit(solution)/shard_map/all_gather | solution.py:73
  268.8 4.6 copy.20
  273.4 296.0 %all-gather.6.cloned.1.call-done = bf16[12288,128]{1,0:T(8,128)(2,1)} async-done(((bf16[192,128]{1,0:T(8,128)(2,1)}), bf16[12288,128]{1,0:T(8,128)(2,1)}) %all-gather.6.cloned.1.call-update) | async-done | bytes 3145744 | tf_op jit(solution)/shard_map/all_gather | solution.py:74
  569.4 300.3 %all-gather.8.cloned.1.call-done = bf16[12288,128]{1,0:T(8,128)(2,1)} async-done(((bf16[192,128]{1,0:T(8,128)(2,1)}), bf16[12288,128]{1,0:T(8,128)(2,1)}) %all-gather.8.cloned.1.call-update) | async-done | bytes 3145744 | tf_op jit(solution)/shard_map/all_gather | solution.py:75
  869.7 162.3 %while.15 = (s32[]{:T(128)}, f32[768,128]{1,0:T(8,128)S(1)}, f32[768,64]{0,1:T(8,128)S(1)}, f32[768]{0:T(1024)S(1)}, f32[768]{0:T(1024)S(1)}, /*index=5*/bf16[12...) while((s32[]{:T(128)}, f32[768,128]{1,0:T(8,128)S(1)}, ...), condition=%wide.region_5.6_spmd.clone, body=%wide.region_1.5_spmd.clone.sunk | while | flops 915160832 | bytes 35353800 | solution.py:97
  870.8 3.5 fusion.88
  874.3 2.7 fusion.89
  880.2 1.5 fusion.92
  884.4 3.5 fusion.88
  887.8 2.7 fusion.89
  897.9 3.5 fusion.88
  901.4 2.7 fusion.89
  907.2 1.5 fusion.92
  911.4 3.5 fusion.88
  914.9 2.7 fusion.89
  924.9 3.5 fusion.88
  928.4 2.7 fusion.89
  934.3 1.5 fusion.92
  938.5 3.5 fusion.88
  941.9 2.7 fusion.89
  947.8 1.5 fusion.92
  952.0 3.5 fusion.88
  955.5 2.7 fusion.89
  961.3 1.5 fusion.92
  965.5 3.5 fusion.88
  969.0 2.7 fusion.89
  974.8 1.5 fusion.92
  979.0 3.5 fusion.88
  982.5 2.7 fusion.89
  988.4 1.5 fusion.92
  992.6 3.5 fusion.88
  996.0 2.7 fusion.89
  1001.9 1.5 fusion.92
  1006.1 3.5 fusion.88
  1009.6 2.7 fusion.89
  1015.4 1.5 fusion.92
  1019.6 3.5 fusion.88
  1023.1 2.7 fusion.89
  1028.9 1.5 fusion.92
  1034.2 53.7 %all-reduce = f32[768]{0:T(1024)S(1)} all-reduce(f32[768]{0:T(1024)S(1)} %get-tuple-element.63), channel_id=3, replica_groups=mesh['enc'=8,'kr'=8,'kc'=4] {'kc'}, use_global_device_ids=true, to_apply=%region_7.8.clone | all-reduce | flops 768 | bytes 6144
  1088.1 21.8 %reduce-scatter.8.cloned.1.call-done = f32[192,64]{1,0:T(8,128)} async-done(((f32[768,64]{1,0:T(8,128)}), f32[192,64]{1,0:T(8,128)}) %reduce-scatter.8.cloned.1.call-update) | async-done | bytes 49168
  1112.2 4.2 convolution_bitcast_fusion
  1116.5 28.4 %reduce-scatter.6.cloned.1.call-done = f32[192,128]{1,0:T(8,128)} async-done(((f32[768,128]{1,0:T(8,128)}), f32[192,128]{1,0:T(8,128)}) %reduce-scatter.6.cloned.1.call-update) | async-done | bytes 98320 | tf_op jit(solution)/shard_map/reduce_scatter | solution.py:44
  1146.4 274.1 %all-reduce.6.cloned.1.call-done = (f32[1024,1024]{0,1:T(8,128)}, f32[1024,64]{1,0:T(8,128)}) async-done(((f32[1024,1024]{0,1:T(8,128)}, f32[1024,64]{1,0:T(8,128)}), (f32[1024,1024]{0,1:T(8,128)}, f32[1024,64]{1,0:T(8,128)})) %all-reduce.6.cloned.1.call-update) | async-done | bytes 4456464
  (133 shorter events, 86.9 us)
Async XLA Ops:
  7.2 1.6 copy-start
  7.2 4.1 copy-start.6
  7.2 4.1 copy-start.7
  7.2 261.6 %all-gather.10.cloned.1.call-start = ((), (), s32[]{:S(2)}) async-start(), calls=%async_computation.5 | async-start | bytes 2129920 | tf_op jit(solution)/shard_map/all_gather | solution.py:73
  8.8 24.2 %copy-start.5 = (bf16[192,128]{1,0:T(8,128)(2,1)S(1)}, bf16[192,128]{1,0:T(8,128)(2,1)}, u32[]{:S(2)}) copy-start(bf16[192,128]{1,0:T(8,128)(2,1)} %param.12) | copy-start | bytes 147460
  12.2 557.2 %all-gather.6.cloned.1.call-start = ((), (), s32[]{:S(2)}) async-start(), calls=%async_computation.2 | async-start | bytes 3194880 | tf_op jit(solution)/shard_map/all_gather | solution.py:74
  13.0 856.7 %all-gather.8.cloned.1.call-start = ((), (), s32[]{:S(2)}) async-start(), calls=%async_computation.3 | async-start | bytes 3194880 | tf_op jit(solution)/shard_map/all_gather | solution.py:75
  13.7 1096.2 %reduce-scatter.8.cloned.1.call-start = ((), (), s32[]{:S(2)}) async-start(), calls=%async_computation.6 | async-start | bytes 491520
  24.2 0.6 copy-start.3
  869.7 163.3 %copy-start.8 = (u32[256]{0:T(256)S(1)}, u32[256]{0:T(256)}, u32[]{:S(2)}) copy-start(u32[256]{0:T(256)} %constant.36) | copy-start | bytes 3076
  869.7 241.3 %copy-start.4 = (bf16[192,64]{0,1:T(8,128)(2,1)S(1)}, bf16[192,64]{0,1:T(8,128)(2,1)}, u32[]{:S(2)}) copy-start(bf16[192,64]{0,1:T(8,128)(2,1)} %fusion.38) | copy-start | bytes 73732
  874.3 2.9 copy-start.1
  887.8 2.9 copy-start.1
  901.4 2.9 copy-start.1
  914.9 2.9 copy-start.1
  928.4 2.9 copy-start.1
  941.9 2.9 copy-start.1
  955.5 2.9 copy-start.1
  969.0 2.9 copy-start.1
  982.5 2.9 copy-start.1
  996.0 2.9 copy-start.1
  1009.6 2.9 copy-start.1
  1023.1 2.9 copy-start.1
  1032.0 56.0 %copy-start.2 = (f32[768,128]{1,0:T(8,128)}, f32[768,128]{1,0:T(8,128)S(1)}, u32[]{:S(2)}) copy-start(f32[768,128]{1,0:T(8,128)S(1)} %get-tuple-element.62) | copy-start | bytes 1179652
  1032.9 112.0 %reduce-scatter.6.cloned.1.call-start = ((), (), s32[]{:S(2)}) async-start(), calls=%async_computation.4 | async-start | bytes 491520 | tf_op jit(solution)/shard_map/reduce_scatter | solution.py:44
  1088.0 332.5 %all-reduce.6.cloned.1.call-start = ((), (), s32[]{:S(2)}) async-start(), calls=%async_computation.7 | async-start | bytes 9437184
Sparse Core Ops, SparseCore 0:
  12.3 256.4 all-gather.9
  270.6 298.7 all-gather.5
  571.2 298.4 all-gather.7
  1033.0 76.8 reduce-scatter.7
  1112.5 32.2 reduce-scatter.5
  1150.2 270.1 all-reduce.5
where the time goes:
time: 1430 us
  waiting for transfers between devices  1150 us (80%)
  matrix products  154 us (11%)
  blocking collectives  78.3 us (5%)
  other arithmetic  16.6 us (1%)
  local copies, waits for them, and re-layouts  15.8 us (1%)
  between operations  14.9 us (1%)
    all_gather x1, waiting for transfers between devices, local(): lax.all_gather(solves, ('enc', 'kr'), axis=0, tiled=True)  300 us
    unnamed x8, waiting for transfers between devices  297 us
    all_gather x1, waiting for transfers between devices, local(): lax.all_gather(probes, ('enc', 'kr'), axis=0, tiled=True)  296 us
    all_gather x1, waiting for transfers between devices, local(): lax.all_gather(scaled, ('enc', 'kr'), axis=0, tiled=True)  228 us
    dot_general x36, matrix products, contract_inner(): lax.dot_general(left, right, (((1,), (1,)), ((), ())), preferred_element_...  78.7 us
    unnamed x1, blocking collectives  53.7 us
    dot_general x12, matrix products, advance(): jnp.dot(kernel.astype(jnp.bfloat16), col_probe, preferred_element_type=jn...  32.7 us
  transfers between devices with their start and end apart: 6, of which 6 were waited for; matrix products, arithmetic and copies ran while one was open for 1% of the time, Pallas kernels for 0%

commit v1 on v0

v1 whole, which is shorter than its diff:
```python
import functools
import math

import jax
import jax.numpy as jnp
from jax import lax
from jax.experimental import pallas as pl
from jax.experimental.pallas import tpu as pltpu
from jax.sharding import PartitionSpec as P

probe_gain = 0.5
loss_gain = 0.02

ROWS = 192
HALF = ROWS // 2
IN = 1024
HID = 1024
FEAT = 64
PROBES = 128
PLANE = 16
COLS = 16
WIDTH = COLS * ROWS
GROUP = 4
SLICE = HID // GROUP
GROWS = GROUP * ROWS
LANES = SLICE // 128
TILES = 8 * LANES + 4
LOG2E = 1.4426950408889634
MESH = pl.DeviceIdType.MESH
f32 = jnp.float32
bf16 = jnp.bfloat16


def dot(left, right):
    return jnp.dot(left, right, preferred_element_type=f32)


def dot_nt(left, right):
    return lax.dot_general(left, right, (((1,), (1,)), ((), ())), preferred_element_type=f32)


def split3(value):
    one = value.astype(bf16)
    rest = value - one.astype(f32)
    two = rest.astype(bf16)
    three = (rest - two.astype(f32)).astype(bf16)
    return one, two, three


def unpack_rows(packed):
    return jnp.concatenate([packed[:, :FEAT], packed[:, FEAT:]], axis=0)


def pack_rows(value):
    half = value.shape[0] // 2
    return jnp.concatenate([value[:half], value[half:]], axis=1)


def half_norms(wide):
    return (-0.5 * LOG2E) * jnp.sum(wide * wide, axis=1, keepdims=True)


def extras(norms, own, other):
    one, two, three = split3(norms)
    lane = lax.broadcasted_iota(jnp.int32, (norms.shape[0], FEAT), 1)
    filled = jnp.where((lane >= other) & (lane < other + 3), 1.0, 0.0)
    filled = jnp.where(lane == own, one.astype(f32), filled)
    filled = jnp.where(lane == own + 1, two.astype(f32), filled)
    filled = jnp.where(lane == own + 2, three.astype(f32), filled)
    return filled.astype(bf16)


def kernel(
    inputs, w_first, w_second, inv_length, probes, solves,
    products, grad_first, grad_second,
    row_p, row_s, row_u, col_p, col_s, col_u, cross_t, inner_t, mix,
    out_v, out_d, got_v, got_d,
    group_x, group_xt, factor, hidden_t, group_d,
    chunks, got_chunks, pieces, got_pieces,
    row_send, row_recv, col_send, col_recv, side_send, side_recv,
    out_send, out_recv, x_send, x_recv, d_send, d_recv,
    chunk_send, chunk_recv, piece_send, piece_recv,
):
    z = lax.axis_index("enc")
    kr = lax.axis_index("kr")
    kc = lax.axis_index("kc")
    y = lax.rem(kr, 4)
    x = 2 * lax.div(kc, 2) + lax.div(kr, 4)
    core = lax.rem(kc, 2)

    def device(x, y, z, core):
        return (z, 4 * lax.rem(x, 2) + y, 2 * lax.div(x, 2) + core)

    def plane_peer(step, sign):
        dx = lax.div(step, 4)
        dy = lax.rem(step, 4)
        px = lax.rem(x + 4 + sign * dx, 4)
        py = lax.rem(y + 4 + sign * dy, 4)
        return px, py

    def column_peer(step):
        return lax.rem(z + lax.div(step, 2), 8), lax.rem(core + lax.rem(step, 2), 2)

    def remote(src, dst, send, recv, target):
        return pltpu.make_async_remote_copy(
            src_ref=src, dst_ref=dst, send_sem=send, recv_sem=recv,
            device_id=target, device_id_type=MESH,
        )

    me = (z, kr, kc)
    sibling = device(x, y, z, 1 - core)
    up = device(x, y, lax.rem(z + 1, 8), core)
    down = device(x, y, lax.rem(z + 7, 8), core)
    z_low = lax.rem(z, 2)
    member = 2 * z_low + core

    barrier = pltpu.get_barrier_semaphore()

    def greet_plane(step, carry):
        px, py = plane_peer(step, 1)
        pl.semaphore_signal(barrier, inc=1, device_id=device(px, py, z, core), device_id_type=MESH)
        return carry

    def greet_column(step, carry):
        pz, pc = column_peer(step)
        pl.semaphore_signal(barrier, inc=1, device_id=device(x, y, pz, pc), device_id_type=MESH)
        return carry

    lax.fori_loop(1, PLANE, greet_plane, 0)
    lax.fori_loop(1, COLS, greet_column, 0)
    pl.semaphore_wait(barrier, 30)

    def ring(which, source, slot, part_up):
        buffers = (col_p, col_s, col_u)
        buffer = buffers[which]
        if part_up and slot < 4:
            yield remote(source, buffer.at[slot + 1], col_send.at[which, slot], col_recv.at[which, slot + 1], up)
        if slot == 0 or 5 <= slot < 7:
            later = 5 if slot == 0 else slot + 1
            yield remote(source, buffer.at[later], col_send.at[which, slot + 4 if slot == 0 else slot], col_recv.at[which, later], down)
        yield remote(source, buffer.at[8 + slot], side_send.at[which, slot], side_recv.at[which, slot], sibling)

    sources = (probes, solves)
    for which in range(2):
        for copy in ring(which, sources[which], 0, True):
            copy.start()

    def row_copy(which, step):
        px, py = plane_peer(step, -1)
        source = (probes, solves, col_u.at[0])[which]
        return remote(
            source, (row_p, row_s, row_u)[which].at[step],
            row_send.at[which, step], row_recv.at[which, step], device(px, py, z, core),
        )

    def send_rows(step, carry):
        row_copy(0, step).start()
        row_copy(1, step).start()
        return carry

    lax.fori_loop(1, PLANE, send_rows, 0)

    def encode(block, total):
        start = pl.multiple_of(block * 256, 256)
        pre = dot(inputs[...], w_first[:, pl.ds(start, 256)])
        hidden = (pre * jax.nn.sigmoid(pre)).astype(bf16)
        hidden_t[pl.ds(start, 256), :] = hidden.T
        return total + dot(hidden, w_second[pl.ds(start, 256), :])

    features = lax.fori_loop(0, HID // 256, encode, jnp.zeros((ROWS, FEAT), f32))
    scaled = (features * inv_length[...]).astype(bf16)
    packed = pack_rows(scaled)
    col_u[0] = packed
    row_u[0] = packed
    for copy in ring(2, col_u.at[0], 0, True):
        copy.start()

    def send_features(step, carry):
        row_copy(2, step).start()
        return carry

    lax.fori_loop(1, PLANE, send_features, 0)

    def group_copy(step, source, buffer, send, recv):
        other = lax.rem(member + step, GROUP)
        pz = z - z_low + lax.div(other, 2)
        return remote(source, buffer.at[member], send.at[step], recv.at[step], device(x, y, pz, lax.rem(other, 2)))

    def group_wait(step, source, buffer, send, recv):
        other = lax.rem(member + GROUP - step, GROUP)
        remote(source, buffer.at[other], send.at[step], recv.at[step], me).wait_recv()

    col_p[0] = probes[...]
    col_s[0] = solves[...]
    row_p[0] = probes[...]
    row_s[0] = solves[...]
    group_x[member] = inputs[...]

    for slot in (1, 5, 2, 6, 3, 7, 4):
        for which in range(3):
            buffer = (col_p, col_s, col_u)[which]
            remote(buffer.at[slot], buffer.at[slot], col_send.at[which, 0], col_recv.at[which, slot], me).wait_recv()
            for copy in ring(which, buffer.at[slot], slot, slot < 5):
                copy.start()
    for step in range(1, GROUP):
        group_copy(step, inputs, group_x, x_send, x_recv).start()
    for slot in range(8):
        for which in range(3):
            buffer = (col_p, col_s, col_u)[which]
            remote(buffer.at[slot], buffer.at[8 + slot], side_send.at[which, slot], side_recv.at[which, slot], me).wait_recv()

    def prepare(pair, carry):
        slot = 2 * pair
        start = pl.multiple_of(slot * ROWS, 2 * ROWS)
        u = jnp.concatenate([unpack_rows(col_u[slot]), unpack_rows(col_u[slot + 1])], axis=0)
        wide = u.astype(f32)
        one, two, three = split3(wide * LOG2E)
        tail = extras(half_norms(wide), 3, 0)
        operand = jnp.concatenate([one, two, three, tail], axis=1)
        cross_t[:, pl.ds(start, 2 * ROWS)] = operand.T
        p = jnp.concatenate([col_p[slot], col_p[slot + 1]], axis=0)
        s = jnp.concatenate([col_s[slot], col_s[slot + 1]], axis=0)
        inner_t[pl.ds(0, PROBES), pl.ds(start, 2 * ROWS)] = p.T
        inner_t[pl.ds(PROBES, PROBES), pl.ds(start, 2 * ROWS)] = s.T
        mix[pl.ds(start, 2 * ROWS), :] = u
        return carry

    lax.fori_loop(0, COLS // 2, prepare, 0)

    def out_copy(step, which):
        px, py = plane_peer(step, 1)
        source = (out_v, out_d)[which]
        target = (got_v, got_d)[which]
        return remote(
            source.at[step], target.at[step], out_send.at[which, step], out_recv.at[which, step],
            device(px, py, z, core),
        )

    def row_block(step, carry):
        @pl.when(step > 0)
        def _():
            for which in range(3):
                row_copy(which, step).wait_recv()

        u = unpack_rows(row_u[step])
        wide = u.astype(f32)
        left = jnp.concatenate([u, u, u, extras(half_norms(wide), 0, 3)], axis=1)
        inner = jnp.concatenate([row_s[step], row_p[step]], axis=1)
        vsum = jnp.zeros((ROWS, PROBES), f32)
        mixed = jnp.zeros((ROWS, FEAT), f32)
        sums = jnp.zeros((ROWS, 2 * FEAT), f32)
        block = 1024
        for start in range(0, WIDTH, block):
            value = jnp.exp2(dot(left, cross_t[:, start:start + block]))
            both = value * dot(inner, inner_t[:, start:start + block])
            for lane in range(0, block, 2 * FEAT):
                sums = sums + both[:, lane:lane + 2 * FEAT]
            both = both.astype(bf16)
            p = col_p[...].reshape(WIDTH, PROBES)[start:start + block]
            vsum = vsum + dot(value.astype(bf16), p)
            mixed = mixed + dot(both, mix[start:start + block, :])
        part = jnp.sum(sums, axis=1, keepdims=True) * wide - mixed
        out_v[step] = vsum.astype(bf16)
        out_d[step] = pack_rows(part).astype(bf16)

        @pl.when(step > 0)
        def _():
            out_copy(step, 0).start()
            out_copy(step, 1).start()

        return carry

    lax.fori_loop(0, PLANE, row_block, 0)

    for step in range(1, GROUP):
        group_wait(step, inputs, group_x, x_send, x_recv)
    here = pl.multiple_of(member * SLICE, SLICE)

    def group_rows(pair, carry):
        rows = group_x[pl.ds(2 * pair, 2)].reshape(2 * ROWS, IN)
        start = pl.multiple_of(pair * 2 * ROWS, 2 * ROWS)
        group_xt[:, pl.ds(start, 2 * ROWS)] = rows.T
        pre = dot(rows, w_first[:, pl.ds(here, SLICE)])
        sigma = jax.nn.sigmoid(pre)
        factor[pl.ds(start, 2 * ROWS), :] = sigma * (1.0 + pre * (1.0 - sigma))
        return carry

    lax.fori_loop(0, GROUP // 2, group_rows, 0)

    def add_up(step, totals):
        for which in range(2):
            out_copy(step, which).wait_recv()
        return totals[0] + got_v[step].astype(f32), totals[1] + got_d[step].astype(f32)

    vsum, part = lax.fori_loop(1, PLANE, add_up, (out_v[0].astype(f32), out_d[0].astype(f32)))
    products[...] = (vsum * probe_gain).astype(bf16)
    lscale = loss_gain / math.sqrt(PROBES)
    length = inv_length[...]
    dfeat = part * (-lscale * jnp.concatenate([length, length], axis=1))
    packed_d = dfeat.astype(bf16)
    group_d[member] = packed_d
    for step in range(1, GROUP):
        group_copy(step, group_d.at[member], group_d, d_send, d_recv).start()

    second = dot(hidden_t[...], unpack_rows(packed_d))
    low = jnp.concatenate([second[: HID // 2], second[HID // 2:]], axis=1).astype(bf16)
    for far in range(4):
        tile = 8 * LANES + far
        chunks[:, tile * 8:tile * 8 + 8, :] = low[128 * far:128 * far + 128].reshape(PLANE, 8, 128)

    for step in range(1, GROUP):
        group_wait(step, group_d.at[member], group_d, d_send, d_recv)
    whole_d = jnp.concatenate([unpack_rows(group_d[item]) for item in range(GROUP)], axis=0)
    back = dot_nt(whole_d, w_second[pl.ds(here, SLICE), :])
    dpre = (back * factor[...]).astype(bf16)
    for far in range(8):
        first = dot(group_xt[128 * far:128 * far + 128, :], dpre).astype(bf16)
        for lane in range(LANES):
            tile = far * LANES + lane
            chunks[:, tile * 8:tile * 8 + 8, :] = first[:, 128 * lane:128 * lane + 128].reshape(PLANE, 8, 128)

    def place(px, py):
        return 2 * (4 * lax.rem(px, 2) + py) + lax.div(px, 2)

    def chunk_copy(step):
        px, py = plane_peer(step, 1)
        return remote(
            chunks.at[place(px, py)], got_chunks.at[step], chunk_send.at[step], chunk_recv.at[step],
            device(px, py, z, core),
        )

    def send_chunk(step, carry):
        chunk_copy(step).start()
        return carry

    lax.fori_loop(1, PLANE, send_chunk, 0)

    def add_chunk(step, total):
        chunk_copy(step).wait_recv()
        return total + got_chunks[step].astype(f32)

    summed = lax.fori_loop(1, PLANE, add_chunk, chunks[place(x, y)].astype(f32))

    depth = 8 * LANES
    for far in range(8):
        extra = 8 * depth + 8 * (far % 4)
        pieces[far] = jnp.concatenate(
            [summed[depth * far:depth * far + depth], summed[extra:extra + 8]], axis=0
        )

    own_slot = 2 * z + core

    def piece_copy(step):
        pz, pc = column_peer(step)
        return remote(
            pieces.at[pz], got_pieces.at[own_slot], piece_send.at[step], piece_recv.at[step],
            device(x, y, pz, pc),
        )

    def send_piece(step, carry):
        piece_copy(step).start()
        return carry

    lax.fori_loop(1, COLS, send_piece, 0)
    got_pieces[own_slot] = pieces[z]

    def wait_piece(step, carry):
        pz = lax.rem(z + 8 - lax.div(step, 2), 8)
        pc = lax.rem(core + lax.rem(step, 2), 2)
        remote(pieces.at[z], got_pieces.at[2 * pz + pc], piece_send.at[step], piece_recv.at[step], me).wait_recv()
        return carry

    lax.fori_loop(1, COLS, wait_piece, 0)
    strips = []
    tail = jnp.zeros((8, 128), f32)
    for item in range(GROUP):
        total = got_pieces[item]
        for other in range(item + GROUP, COLS, GROUP):
            total = total + got_pieces[other]
        strips += [total[8 * lane:8 * lane + 8] for lane in range(LANES)]
        tail = tail + total[depth:depth + 8]
    full = jnp.concatenate(strips, axis=1)
    grad_first[...] = jnp.where(core == 0, full[:4], full[4:])
    tail = jnp.where(z < 4, tail[:, :FEAT], tail[:, FEAT:])
    grad_second[...] = jnp.where(core == 0, tail[:4], tail[4:])

    for which in range(3):
        source = (probes, solves, col_u.at[0])[which]
        for copy in ring(which, source, 0, True):
            copy.wait_send()
        for slot in range(1, 8):
            for copy in ring(which, (col_p, col_s, col_u)[which].at[slot], slot, slot < 5):
                copy.wait_send()

    def finish_plane(step, carry):
        for which in range(3):
            row_copy(which, step).wait_send()
        for which in range(2):
            out_copy(step, which).wait_send()
        chunk_copy(step).wait_send()
        return carry

    lax.fori_loop(1, PLANE, finish_plane, 0)
    for step in range(1, GROUP):
        group_copy(step, inputs, group_x, x_send, x_recv).wait_send()
        group_copy(step, group_d.at[member], group_d, d_send, d_recv).wait_send()

    def finish_column(step, carry):
        piece_copy(step).wait_send()
        return carry

    lax.fori_loop(1, COLS, finish_column, 0)


def local(inputs, w_first, w_second, inv_length, probes, solves):
    vmem = pl.BlockSpec(memory_space=pltpu.VMEM)
    dma = pltpu.SemaphoreType.DMA
    return pl.pallas_call(
        kernel,
        out_shape=(
            jax.ShapeDtypeStruct((ROWS, PROBES), bf16),
            jax.ShapeDtypeStruct((4, HID), f32),
            jax.ShapeDtypeStruct((4, FEAT), f32),
        ),
        in_specs=[vmem] * 6,
        out_specs=(vmem, vmem, vmem),
        scratch_shapes=[
            pltpu.VMEM((PLANE, ROWS, PROBES), bf16),
            pltpu.VMEM((PLANE, ROWS, PROBES), bf16),
            pltpu.VMEM((PLANE, HALF, 2 * FEAT), bf16),
            pltpu.VMEM((COLS, ROWS, PROBES), bf16),
            pltpu.VMEM((COLS, ROWS, PROBES), bf16),
            pltpu.VMEM((COLS, HALF, 2 * FEAT), bf16),
            pltpu.VMEM((4 * FEAT, WIDTH), bf16),
            pltpu.VMEM((2 * PROBES, WIDTH), bf16),
            pltpu.VMEM((WIDTH, FEAT), bf16),
            pltpu.VMEM((PLANE, ROWS, PROBES), bf16),
            pltpu.VMEM((PLANE, HALF, 2 * FEAT), bf16),
            pltpu.VMEM((PLANE, ROWS, PROBES), bf16),
            pltpu.VMEM((PLANE, HALF, 2 * FEAT), bf16),
            pltpu.VMEM((GROUP, ROWS, IN), bf16),
            pltpu.VMEM((IN, GROWS), bf16),
            pltpu.VMEM((GROWS, SLICE), f32),
            pltpu.VMEM((HID, ROWS), bf16),
            pltpu.VMEM((GROUP, HALF, 2 * FEAT), bf16),
            pltpu.VMEM((PLANE, TILES * 8, 128), bf16),
            pltpu.VMEM((PLANE, TILES * 8, 128), bf16),
            pltpu.VMEM((8, 8 * LANES + 8, 128), f32),
            pltpu.VMEM((COLS, 8 * LANES + 8, 128), f32),
            dma((3, PLANE)), dma((3, PLANE)),
            dma((3, 8)), dma((3, 8)), dma((3, 8)), dma((3, 8)),
            dma((2, PLANE)), dma((2, PLANE)),
            dma((GROUP,)), dma((GROUP,)), dma((GROUP,)), dma((GROUP,)),
            dma((PLANE,)), dma((PLANE,)), dma((COLS,)), dma((COLS,)),
        ],
        compiler_params=pltpu.CompilerParams(
            collective_id=0, has_side_effects=True, vmem_limit_bytes=56 * 1024 * 1024
        ),
        name="gradient_step",
    )(inputs, w_first, w_second, inv_length.reshape(1, FEAT), probes, solves)


def solution(mesh):
    rows = P(("enc", "kr", "kc"), None)
    return jax.shard_map(
        local, mesh=mesh, in_specs=(rows, P(), P(), P(), rows, rows),
        out_specs=(rows, rows, rows), check_vma=False,
    )
```

time: 1430 us -> 95.2 us (0.07)
  waiting for transfers between devices: 1150 us -> 0 us
  matrix products: 154 us -> 0 us
  Pallas kernels: 0 us -> 88.6 us
  blocking collectives: 78.3 us -> 0 us
  other arithmetic: 16.6 us -> 0 us
    all_gather x3 -> x0, waiting for transfers between devices: 824 us -> none  [the longest x1 300 us: local(): lax.all_gather(solves, ('enc', 'kr'), axis=0, tiled=True)]
    unnamed x8 -> x0, waiting for transfers between devices: 297 us -> none
    dot_general x76 -> x0, matrix products: 154 us -> none  [the longest x36 78.7 us: contract_inner(): lax.dot_general(left, right, (((1,), (1,)), ((), ())), preferred_element_...]
    pallas_call x0 -> x1, Pallas kernels: none -> 88.6 us  [local(): pl.pallas_call(kernel, out_shape=(jax.ShapeDtypeStruct((ROWS, PROBES), bf...]
    unnamed x1 -> x0, blocking collectives: 53.7 us -> none
    reduce_scatter x1 -> x0, waiting for transfers between devices: 28.4 us -> none  [row_totals(): lax.psum_scatter(parts[0], 'kc', scatter_dimension=0, tiled=True)]
    all_gather x3 -> x0, blocking collectives: 24.6 us -> none  [the longest x1 10.2 us: local(): lax.all_gather(scaled, 'kc', axis=0, tiled=True)]
    reduce_sum x13 -> x0, other arithmetic: 14.9 us -> none  [the longest x12 14 us: kernel_tile(): col_norm = jnp.sum(col_wide * col_wide, axis=1)]
  transfers between devices with their start and end apart: 6 -> 0, of which waited for: 6 -> 0; matrix products, arithmetic and copies ran while one was open for 1% -> 0% of each run, Pallas kernels for 0% -> 0%
where the time goes in v1:
time: 95.2 us; the launch traced here: 94.9 us
  Pallas kernels  88.6 us (93%)
  local copies, waits for them, and re-layouts  5.74 us (6%)
    pallas_call x1, Pallas kernels, local(): pl.pallas_call(kernel, out_shape=(jax.ShapeDtypeStruct((ROWS, PROBES), bf...  88.6 us
    unnamed x4, local copies, waits for them, and re-layouts  5.74 us

profile of v1, /device:TPU:1, one launch (start us, length us, event | category | flops | bytes accessed | tf_op | source)
XLA Modules:
  0.0 94.9 jit_solution(11783569311623143481)
XLA Ops:
  0.6 1.7 %copy.9.w_second = bf16[1024,64]{1,0:T(8,128)(2,1)} copy(bf16[1024,64]{0,1:T(8,128)(2,1)} %param.8) | data formatting | bytes 262144 | tf_op args[2]
  2.4 88.6 %gradient_step.1 = (bf16[192,128]{1,0:T(8,128)(2,1)}, f32[4,1024]{1,0:T(4,128)}, f32[4,64]{1,0:T(4,128)}) custom-call(bf16[192,1024]{1,0:T(8,128)(2,1)} %inputs.1, bf16[1024,1024]{1,0:T(8,128)(2,1)} %w_first.1, bf16[1024,64]{1,0:T(8,128)(2,1)} %copy.9.w_second, f32[1,64]{1,0:T(1,128)} %bitcast.1, bf16[192,128]{1,0:T(8,128)(2,1)} %probes.1, ...), custom_call_target="tpu_custom_call" | custom-call | tf_op jit(solution)/shard_map/gradient_step/pallas_call | solution.py:418
  90.9 1.4 %copy.13 = bf16[192,128]{1,0:T(8,128)(2,1)} copy(bf16[192,128]{1,0:T(8,128)(2,1)} %get-tuple-element.6) | data formatting | bytes 98304
  92.4 1.3 %copy.14 = f32[4,1024]{1,0:T(4,128)} copy(f32[4,1024]{1,0:T(4,128)} %get-tuple-element.7) | data formatting | bytes 32768
  93.7 1.3 %copy.15 = f32[4,64]{1,0:T(4,128)} copy(f32[4,64]{1,0:T(4,128)} %get-tuple-element.8) | data formatting | bytes 2048

commit v2 on v1

--- a/solution.py
+++ b/solution.py
@@ -35,6 +35,17 @@
     return jnp.dot(left, right, preferred_element_type=f32)
 
 
+NEAR = 5
+EARLY = 5
+STEPS = (
+    (0, 0), (0, 1), (0, 3), (1, 0), (3, 0), (1, 1), (3, 3), (1, 3),
+    (3, 1), (0, 2), (2, 0), (2, 1), (2, 3), (1, 2), (3, 2), (2, 2),
+)
+PAIR = 2 * ROWS
+CHUNK = 4 * ROWS
+OWN = 12
+
+
 def dot_nt(left, right):
     return lax.dot_general(left, right, (((1,), (1,)), ((), ())), preferred_element_type=f32)
 
@@ -71,13 +82,13 @@
 
 
 def kernel(
-    inputs, w_first, w_second, inv_length, probes, solves,
+    inputs_hbm, w_first_hbm, w_second_hbm, inv_length, probes_hbm, solves_hbm,
     products, grad_first, grad_second,
-    row_p, row_s, row_u, col_p, col_s, col_u, cross_t, inner_t, mix,
-    out_v, out_d, got_v, got_d,
+    w_first, w_second, row_p, row_s, row_u, col_p, col_s, col_u, cross_t, inner_t, mix,
+    left_near, near_v, near_m, near_s, out_v, out_d, got_v, got_d,
     group_x, group_xt, factor, hidden_t, group_d,
     chunks, got_chunks, pieces, got_pieces,
-    row_send, row_recv, col_send, col_recv, side_send, side_recv,
+    load_sem, row_send, row_recv, up_send, down_send, side_send, col_recv,
     out_send, out_recv, x_send, x_recv, d_send, d_recv,
     chunk_send, chunk_recv, piece_send, piece_recv,
 ):
@@ -91,12 +102,11 @@
     def device(x, y, z, core):
         return (z, 4 * lax.rem(x, 2) + y, 2 * lax.div(x, 2) + core)
 
+    def moved(dx, dy, sign):
+        return lax.rem(x + 4 + sign * dx, 4), lax.rem(y + 4 + sign * dy, 4)
+
     def plane_peer(step, sign):
-        dx = lax.div(step, 4)
-        dy = lax.rem(step, 4)
-        px = lax.rem(x + 4 + sign * dx, 4)
-        py = lax.rem(y + 4 + sign * dy, 4)
-        return px, py
+        return moved(lax.div(step, 4), lax.rem(step, 4), sign)
 
     def column_peer(step):
         return lax.rem(z + lax.div(step, 2), 8), lax.rem(core + lax.rem(step, 2), 2)
@@ -128,58 +138,151 @@
 
     lax.fori_loop(1, PLANE, greet_plane, 0)
     lax.fori_loop(1, COLS, greet_column, 0)
-    pl.semaphore_wait(barrier, 30)
-
-    def ring(which, source, slot, part_up):
-        buffers = (col_p, col_s, col_u)
-        buffer = buffers[which]
-        if part_up and slot < 4:
-            yield remote(source, buffer.at[slot + 1], col_send.at[which, slot], col_recv.at[which, slot + 1], up)
-        if slot == 0 or 5 <= slot < 7:
-            later = 5 if slot == 0 else slot + 1
-            yield remote(source, buffer.at[later], col_send.at[which, slot + 4 if slot == 0 else slot], col_recv.at[which, later], down)
-        yield remote(source, buffer.at[8 + slot], side_send.at[which, slot], side_recv.at[which, slot], sibling)
-
-    sources = (probes, solves)
-    for which in range(2):
-        for copy in ring(which, sources[which], 0, True):
-            copy.start()
-
-    def row_copy(which, step):
-        px, py = plane_peer(step, -1)
-        source = (probes, solves, col_u.at[0])[which]
-        return remote(
-            source, (row_p, row_s, row_u)[which].at[step],
-            row_send.at[which, step], row_recv.at[which, step], device(px, py, z, core),
-        )
-
-    def send_rows(step, carry):
-        row_copy(0, step).start()
-        row_copy(1, step).start()
-        return carry
-
-    lax.fori_loop(1, PLANE, send_rows, 0)
+
+    loads = [
+        pltpu.make_async_copy(source, target, load_sem.at[index])
+        for index, (source, target) in enumerate((
+            (inputs_hbm, group_x.at[member]), (w_first_hbm, w_first), (w_second_hbm, w_second),
+            (probes_hbm, col_p.at[OWN]), (solves_hbm, col_s.at[OWN]),
+            (probes_hbm, row_p.at[0]), (solves_hbm, row_s.at[0]),
+        ))
+    ]
+    for load in loads:
+        load.start()
+    for load in loads:
+        load.wait()
 
     def encode(block, total):
         start = pl.multiple_of(block * 256, 256)
-        pre = dot(inputs[...], w_first[:, pl.ds(start, 256)])
+        pre = dot(group_x[member], w_first[:, pl.ds(start, 256)])
         hidden = (pre * jax.nn.sigmoid(pre)).astype(bf16)
         hidden_t[pl.ds(start, 256), :] = hidden.T
-        return total + dot(hidden, w_second[pl.ds(start, 256), :])
+        return total + dot_nt(hidden, w_second[:, pl.ds(start, 256)])
 
     features = lax.fori_loop(0, HID // 256, encode, jnp.zeros((ROWS, FEAT), f32))
     scaled = (features * inv_length[...]).astype(bf16)
     packed = pack_rows(scaled)
-    col_u[0] = packed
+    col_u[OWN] = packed
     row_u[0] = packed
-    for copy in ring(2, col_u.at[0], 0, True):
-        copy.start()
-
-    def send_features(step, carry):
-        row_copy(2, step).start()
-        return carry
-
-    lax.fori_loop(1, PLANE, send_features, 0)
+
+    pl.semaphore_wait(barrier, 30)
+
+    columns = (col_u, col_p, col_s)
+    rows = (row_u, row_p, row_s)
+
+    def up_slot(far):
+        if isinstance(far, int):
+            return (OWN, 0, 4, 8, OWN + 2)[far]
+        return jnp.where(far == 4, OWN + 2, 4 * far - 4)
+
+    def down_slot(far):
+        if isinstance(far, int):
+            return (OWN, 1, 5, 9)[far]
+        return 4 * far - 3
+
+    def up_copy(which, far):
+        buffer = columns[which]
+        return remote(
+            buffer.at[up_slot(far)], buffer.at[up_slot(far + 1)],
+            up_send.at[which, far], col_recv.at[which, up_slot(far + 1)], up,
+        )
+
+    def down_copy(which, far):
+        buffer = columns[which]
+        return remote(
+            buffer.at[down_slot(far)], buffer.at[down_slot(far + 1)],
+            down_send.at[which, far], col_recv.at[which, down_slot(far + 1)], down,
+        )
+
+    def side_copy(which, slot, there):
+        buffer = columns[which]
+        return remote(
+            buffer.at[slot], buffer.at[there], side_send.at[which, slot], col_recv.at[which, there], sibling,
+        )
+
+    def column_wait(which, slot):
+        buffer = columns[which]
+        remote(buffer.at[slot], buffer.at[slot], side_send.at[which, 0], col_recv.at[which, slot], me).wait_recv()
+
+    def row_send_on(which, source, dx, dy, here):
+        slot = STEPS.index(here)
+        px, py = moved(dx, dy, 1)
+        return remote(
+            rows[which].at[STEPS.index(source)], rows[which].at[slot],
+            row_send.at[which, slot], row_recv.at[which, slot], device(px, py, z, core),
+        )
+
+    def row_wait(which, step):
+        remote(
+            rows[which].at[0], rows[which].at[step],
+            row_send.at[which, step], row_recv.at[which, step], me,
+        ).wait_recv()
+
+    ways = ((1, 3), (1, 1), (0, 3))
+
+    def offset(axis, along, across):
+        return (along, across) if axis == 0 else (across, along)
+
+    def spread(which, block):
+        first, turn = ways[which]
+        second = 1 - first
+        along, across = block[first], block[second]
+        moves = []
+        if across == 0:
+            if along == 0:
+                moves += [(first, 1), (first, 3)]
+            elif along == (4 - turn) % 4:
+                moves.append((first, turn))
+            moves += [(second, 1), (second, 3)]
+        elif across == (4 - turn) % 4:
+            moves.append((second, turn))
+        for axis, way in moves:
+            here = [block[0], block[1]]
+            here[axis] = (here[axis] - way) % 4
+            row_send_on(which, block, *offset(axis, way, 0), tuple(here)).start()
+
+    waited = set()
+
+    def take(which, block):
+        waited.add((which, block))
+        row_wait(which, STEPS.index(block))
+        spread(which, block)
+
+    def wave(level):
+        for which in range(3):
+            for block in STEPS[1:]:
+                first, turn = ways[which]
+                far = [0 if item == 0 else 2 if item == 2 else 1 for item in block]
+                goes_on = block[1 - first] == 0 or block[1 - first] == (4 - turn) % 4
+                if sum(far) == level and goes_on:
+                    take(which, block)
+
+    for which in range(3):
+        up_copy(which, 0).start()
+        down_copy(which, 0).start()
+        spread(which, (0, 0))
+        side_copy(which, OWN, OWN + 1).start()
+
+    def advance(far):
+        for which in range(3):
+            here = up_slot(far)
+            column_wait(which, here)
+
+            @pl.when(far < 4)
+            def _():
+                up_copy(which, far).start()
+
+            side_copy(which, here, jnp.where(far == 4, OWN + 3, 4 * far - 2)).start()
+
+            @pl.when(far < 4)
+            def _():
+                column_wait(which, down_slot(far))
+
+                @pl.when(far < 3)
+                def _():
+                    down_copy(which, far).start()
+
+                side_copy(which, down_slot(far), 4 * far - 1).start()
 
     def group_copy(step, source, buffer, send, recv):
         other = lax.rem(member + step, GROUP)
@@ -190,45 +293,78 @@
         other = lax.rem(member + GROUP - step, GROUP)
         remote(source, buffer.at[other], send.at[step], recv.at[step], me).wait_recv()
 
-    col_p[0] = probes[...]
-    col_s[0] = solves[...]
-    row_p[0] = probes[...]
-    row_s[0] = solves[...]
-    group_x[member] = inputs[...]
-
-    for slot in (1, 5, 2, 6, 3, 7, 4):
+    inputs = group_x.at[member]
+
+    def row_operand(step):
+        wide = unpack_rows(row_u[step]).astype(f32)
+        u = wide.astype(bf16)
+        return jnp.concatenate([u, u, u, extras(half_norms(wide), 0, 3)], axis=1), wide
+
+    near_v[...] = jnp.zeros_like(near_v)
+    near_m[...] = jnp.zeros_like(near_m)
+    near_s[...] = jnp.zeros_like(near_s)
+    wave(1)
+    advance(1)
+    for block in STEPS[1:NEAR]:
         for which in range(3):
-            buffer = (col_p, col_s, col_u)[which]
-            remote(buffer.at[slot], buffer.at[slot], col_send.at[which, 0], col_recv.at[which, slot], me).wait_recv()
-            for copy in ring(which, buffer.at[slot], slot, slot < 5):
-                copy.start()
-    for step in range(1, GROUP):
-        group_copy(step, inputs, group_x, x_send, x_recv).start()
-    for slot in range(8):
-        for which in range(3):
-            buffer = (col_p, col_s, col_u)[which]
-            remote(buffer.at[slot], buffer.at[8 + slot], side_send.at[which, slot], side_recv.at[which, slot], me).wait_recv()
-
-    def prepare(pair, carry):
+            if (which, block) not in waited:
+                take(which, block)
+
+    def near_row(step, carry):
+        left_near[pl.ds(pl.multiple_of(step * ROWS, ROWS), ROWS), :] = row_operand(step)[0]
+        return carry
+
+    lax.fori_loop(0, NEAR, near_row, 0)
+
+    def prepare(pair):
         slot = 2 * pair
-        start = pl.multiple_of(slot * ROWS, 2 * ROWS)
+        start = pl.multiple_of(slot * ROWS, PAIR)
         u = jnp.concatenate([unpack_rows(col_u[slot]), unpack_rows(col_u[slot + 1])], axis=0)
         wide = u.astype(f32)
         one, two, three = split3(wide * LOG2E)
         tail = extras(half_norms(wide), 3, 0)
         operand = jnp.concatenate([one, two, three, tail], axis=1)
-        cross_t[:, pl.ds(start, 2 * ROWS)] = operand.T
+        cross_t[:, pl.ds(start, PAIR)] = operand.T
         p = jnp.concatenate([col_p[slot], col_p[slot + 1]], axis=0)
         s = jnp.concatenate([col_s[slot], col_s[slot + 1]], axis=0)
-        inner_t[pl.ds(0, PROBES), pl.ds(start, 2 * ROWS)] = p.T
-        inner_t[pl.ds(PROBES, PROBES), pl.ds(start, 2 * ROWS)] = s.T
-        mix[pl.ds(start, 2 * ROWS), :] = u
-        return carry
-
-    lax.fori_loop(0, COLS // 2, prepare, 0)
+        inner_t[pl.ds(0, PROBES), pl.ds(start, PAIR)] = p.T
+        inner_t[pl.ds(PROBES, PROBES), pl.ds(start, PAIR)] = s.T
+        mix[pl.ds(start, PAIR), :] = u
+
+    def tile(left, inner, start, size, p, u):
+        value = jnp.exp2(dot(left, cross_t[:, pl.ds(start, size)]))
+        both = value * dot(inner, inner_t[:, pl.ds(start, size)])
+        sums = both[:, :128]
+        for lane in range(128, size, 128):
+            sums = sums + both[:, lane:lane + 128]
+        return dot(value.astype(bf16), p), dot(both.astype(bf16), u), sums
+
+    def near_tile(low, high, chunk):
+        size = (high - low) * ROWS
+        here = pl.ds(low * ROWS, size)
+        start = pl.multiple_of(chunk * CHUNK, CHUNK)
+        inner = jnp.concatenate(
+            [row_s[low:high].reshape(size, PROBES), row_p[low:high].reshape(size, PROBES)], axis=1
+        )
+        p = col_p[pl.ds(4 * chunk, 4)].reshape(CHUNK, PROBES)
+        vsum, mixed, sums = tile(left_near[here, :], inner, start, CHUNK, p, mix[pl.ds(start, CHUNK), :])
+        near_v[here, :] += vsum
+        near_m[here, :] += mixed
+        near_s[here, :] += sums
+
+    def table(step, values):
+        if isinstance(step, int):
+            return values[step]
+        total = 0
+        for index, value in enumerate(values):
+            if value:
+                total = total + jnp.where(step == index, value, 0)
+        return total
 
     def out_copy(step, which):
-        px, py = plane_peer(step, 1)
+        dx = table(step, [item[0] for item in STEPS])
+        dy = table(step, [item[1] for item in STEPS])
+        px, py = moved(dx, dy, 1)
         source = (out_v, out_d)[which]
         target = (got_v, got_d)[which]
         return remote(
@@ -236,29 +372,7 @@
             device(px, py, z, core),
         )
 
-    def row_block(step, carry):
-        @pl.when(step > 0)
-        def _():
-            for which in range(3):
-                row_copy(which, step).wait_recv()
-
-        u = unpack_rows(row_u[step])
-        wide = u.astype(f32)
-        left = jnp.concatenate([u, u, u, extras(half_norms(wide), 0, 3)], axis=1)
-        inner = jnp.concatenate([row_s[step], row_p[step]], axis=1)
-        vsum = jnp.zeros((ROWS, PROBES), f32)
-        mixed = jnp.zeros((ROWS, FEAT), f32)
-        sums = jnp.zeros((ROWS, 2 * FEAT), f32)
-        block = 1024
-        for start in range(0, WIDTH, block):
-            value = jnp.exp2(dot(left, cross_t[:, start:start + block]))
-            both = value * dot(inner, inner_t[:, start:start + block])
-            for lane in range(0, block, 2 * FEAT):
-                sums = sums + both[:, lane:lane + 2 * FEAT]
-            both = both.astype(bf16)
-            p = col_p[...].reshape(WIDTH, PROBES)[start:start + block]
-            vsum = vsum + dot(value.astype(bf16), p)
-            mixed = mixed + dot(both, mix[start:start + block, :])
+    def finish_rows(step, vsum, mixed, sums, wide):
         part = jnp.sum(sums, axis=1, keepdims=True) * wide - mixed
         out_v[step] = vsum.astype(bf16)
         out_d[step] = pack_rows(part).astype(bf16)
@@ -268,9 +382,85 @@
             out_copy(step, 0).start()
             out_copy(step, 1).start()
 
-        return carry
-
-    lax.fori_loop(0, PLANE, row_block, 0)
+    def near_out(step, carry):
+        here = pl.ds(pl.multiple_of(step * ROWS, ROWS), ROWS)
+        wide = unpack_rows(row_u[step]).astype(f32)
+        finish_rows(step, near_v[here, :], near_m[here, :], near_s[here, :], wide)
+        return carry
+
+    def near_chunk(far, carry):
+        @pl.when(far <= 4)
+        def _():
+            for which in range(3):
+                @pl.when(far < 4)
+                def _():
+                    column_wait(which, 4 * far - 2)
+                    column_wait(which, 4 * far - 1)
+
+                @pl.when(far == 4)
+                def _():
+                    column_wait(which, OWN + 1)
+                    column_wait(which, OWN + 3)
+
+            prepare(2 * far - 2)
+            prepare(2 * far - 1)
+            near_tile(0, NEAR, far - 1)
+
+        @pl.when(far == 4)
+        def _():
+            lax.fori_loop(0, NEAR, near_out, 0)
+
+        @pl.when(far < 4)
+        def _():
+            advance(far + 1)
+
+        @pl.when(far == 1)
+        def _():
+            wave(2)
+
+        @pl.when(far == 2)
+        def _():
+            wave(3)
+
+        @pl.when(far == 3)
+        def _():
+            for block in STEPS[NEAR:EARLY]:
+                for which in range(3):
+                    if (which, block) not in waited:
+                        take(which, block)
+            lax.fori_loop(NEAR, EARLY, near_row, 0)
+
+        if EARLY > NEAR:
+            @pl.when(far >= 3)
+            def _():
+                near_tile(NEAR, EARLY, far - 3)
+
+        return carry
+
+    lax.fori_loop(1, 7 if EARLY > NEAR else 5, near_chunk, 0)
+    for block in STEPS[1:]:
+        for which in range(3):
+            if (which, block) not in waited:
+                take(which, block)
+    for step in range(1, GROUP):
+        group_copy(step, inputs, group_x, x_send, x_recv).start()
+
+    lax.fori_loop(NEAR, EARLY, near_out, 0)
+
+    def row_block(index, carry):
+        step = PLANE - 1 - index
+        left, wide = row_operand(step)
+        inner = jnp.concatenate([row_s[step], row_p[step]], axis=1)
+        total = None
+        block = 1024
+        for start in range(0, WIDTH, block):
+            p = col_p[...].reshape(WIDTH, PROBES)[start:start + block]
+            part = tile(left, inner, start, block, p, mix[start:start + block, :])
+            total = part if total is None else tuple(a + b for a, b in zip(total, part))
+        finish_rows(step, *total, wide)
+        return carry
+
+    lax.fori_loop(0, PLANE - EARLY, row_block, 0)
 
     for step in range(1, GROUP):
         group_wait(step, inputs, group_x, x_send, x_recv)
@@ -311,7 +501,7 @@
     for step in range(1, GROUP):
         group_wait(step, group_d.at[member], group_d, d_send, d_recv)
     whole_d = jnp.concatenate([unpack_rows(group_d[item]) for item in range(GROUP)], axis=0)
-    back = dot_nt(whole_d, w_second[pl.ds(here, SLICE), :])
+    back = dot(whole_d, w_second[:, pl.ds(here, SLICE)])
     dpre = (back * factor[...]).astype(bf16)
     for far in range(8):
         first = dot(group_xt[128 * far:128 * far + 128, :], dpre).astype(bf16)
@@ -346,7 +536,7 @@
         extra = 8 * depth + 8 * (far % 4)
         pieces[far] = jnp.concatenate(
             [summed[depth * far:depth * far + depth], summed[extra:extra + 8]], axis=0
-        )
+        ).astype(bf16)
 
     own_slot = 2 * z + core
 
@@ -374,9 +564,9 @@
     strips = []
     tail = jnp.zeros((8, 128), f32)
     for item in range(GROUP):
-        total = got_pieces[item]
+        total = got_pieces[item].astype(f32)
         for other in range(item + GROUP, COLS, GROUP):
-            total = total + got_pieces[other]
+            total = total + got_pieces[other].astype(f32)
         strips += [total[8 * lane:8 * lane + 8] for lane in range(LANES)]
         tail = tail + total[depth:depth + 8]
     full = jnp.concatenate(strips, axis=1)
@@ -385,16 +575,19 @@
     grad_second[...] = jnp.where(core == 0, tail[:4], tail[4:])
 
     for which in range(3):
-        source = (probes, solves, col_u.at[0])[which]
-        for copy in ring(which, source, 0, True):
-            copy.wait_send()
-        for slot in range(1, 8):
-            for copy in ring(which, (col_p, col_s, col_u)[which].at[slot], slot, slot < 5):
-                copy.wait_send()
+        for far in range(4):
+            up_copy(which, far).wait_send()
+        for far in range(3):
+            down_copy(which, far).wait_send()
+        for slot in (0, 1, 4, 5, 8, 9, OWN, OWN + 2):
+            side_copy(which, slot, 2).wait_send()
 
     def finish_plane(step, carry):
         for which in range(3):
-            row_copy(which, step).wait_send()
+            remote(
+                rows[which].at[0], rows[which].at[step],
+                row_send.at[which, step], row_recv.at[which, step], me,
+            ).wait_send()
         for which in range(2):
             out_copy(step, which).wait_send()
         chunk_copy(step).wait_send()
@@ -412,19 +605,29 @@
     lax.fori_loop(1, COLS, finish_column, 0)
 
 
+def settle(products, grad_first, grad_second, out_products, out_first, out_second):
+    out_products[...] = products[...]
+    out_first[...] = grad_first[...]
+    out_second[...] = grad_second[...]
+
+
 def local(inputs, w_first, w_second, inv_length, probes, solves):
     vmem = pl.BlockSpec(memory_space=pltpu.VMEM)
+    hbm = pl.BlockSpec(memory_space=pl.ANY)
     dma = pltpu.SemaphoreType.DMA
-    return pl.pallas_call(
+    shapes = (
+        jax.ShapeDtypeStruct((ROWS, PROBES), bf16),
+        jax.ShapeDtypeStruct((4, HID), f32),
+        jax.ShapeDtypeStruct((4, FEAT), f32),
+    )
+    results = pl.pallas_call(
         kernel,
-        out_shape=(
-            jax.ShapeDtypeStruct((ROWS, PROBES), bf16),
-            jax.ShapeDtypeStruct((4, HID), f32),
-            jax.ShapeDtypeStruct((4, FEAT), f32),
-        ),
-        in_specs=[vmem] * 6,
+        out_shape=shapes,
+        in_specs=[hbm, hbm, hbm, vmem, hbm, hbm],
         out_specs=(vmem, vmem, vmem),
         scratch_shapes=[
+            pltpu.VMEM((IN, HID), bf16),
+            pltpu.VMEM((FEAT, HID), bf16),
             pltpu.VMEM((PLANE, ROWS, PROBES), bf16),
             pltpu.VMEM((PLANE, ROWS, PROBES), bf16),
             pltpu.VMEM((PLANE, HALF, 2 * FEAT), bf16),
@@ -434,6 +637,10 @@
             pltpu.VMEM((4 * FEAT, WIDTH), bf16),
             pltpu.VMEM((2 * PROBES, WIDTH), bf16),
             pltpu.VMEM((WIDTH, FEAT), bf16),
+            pltpu.VMEM((EARLY * ROWS, 4 * FEAT), bf16),
+            pltpu.VMEM((EARLY * ROWS, PROBES), f32),
+            pltpu.VMEM((EARLY * ROWS, FEAT), f32),
+            pltpu.VMEM((EARLY * ROWS, 128), f32),
             pltpu.VMEM((PLANE, ROWS, PROBES), bf16),
             pltpu.VMEM((PLANE, HALF, 2 * FEAT), bf16),
             pltpu.VMEM((PLANE, ROWS, PROBES), bf16),
@@ -445,10 +652,10 @@
             pltpu.VMEM((GROUP, HALF, 2 * FEAT), bf16),
             pltpu.VMEM((PLANE, TILES * 8, 128), bf16),
             pltpu.VMEM((PLANE, TILES * 8, 128), bf16),
-            pltpu.VMEM((8, 8 * LANES + 8, 128), f32),
-            pltpu.VMEM((COLS, 8 * LANES + 8, 128), f32),
-            dma((3, PLANE)), dma((3, PLANE)),
-            dma((3, 8)), dma((3, 8)), dma((3, 8)), dma((3, 8)),
+            pltpu.VMEM((8, 8 * LANES + 8, 128), bf16),
+            pltpu.VMEM((COLS, 8 * LANES + 8, 128), bf16),
+            dma((7,)), dma((3, PLANE)), dma((3, PLANE)),
+            dma((3, 4)), dma((3, 4)), dma((3, COLS)), dma((3, COLS)),
             dma((2, PLANE)), dma((2, PLANE)),
             dma((GROUP,)), dma((GROUP,)), dma((GROUP,)), dma((GROUP,)),
             dma((PLANE,)), dma((PLANE,)), dma((COLS,)), dma((COLS,)),
@@ -457,7 +664,10 @@
             collective_id=0, has_side_effects=True, vmem_limit_bytes=56 * 1024 * 1024
         ),
         name="gradient_step",
-    )(inputs, w_first, w_second, inv_length.reshape(1, FEAT), probes, solves)
+    )(inputs, w_first, w_second.T, inv_length.reshape(1, FEAT), probes, solves)
+    return pl.pallas_call(
+        settle, out_shape=shapes, in_specs=[vmem] * 3, out_specs=(vmem, vmem, vmem), name="settle"
+    )(*results)
 
 
 def solution(mesh):

time: 95.2 us -> 83.6 us (0.88)
  Pallas kernels: 88.6 us -> 82.8 us
  local copies, waits for them, and re-layouts: 5.74 us -> 0 us
    pallas_call x1 -> x2, Pallas kernels: 88.6 us -> 82.8 us  [the longest x1 81.3 us: local(): pl.pallas_call(kernel, out_shape=shapes, in_specs=[hbm, hbm, hbm, vmem, h...]
    unnamed x4 -> x0, local copies, waits for them, and re-layouts: 5.74 us -> none
where the time goes in v2:
time: 83.6 us; the launch traced here: 83.4 us
  Pallas kernels  82.8 us (99%)
    pallas_call x1, Pallas kernels, local(): pl.pallas_call(kernel, out_shape=shapes, in_specs=[hbm, hbm, hbm, vmem, h...  81.3 us

profile of v2, /device:TPU:1, one launch (start us, length us, event | category | flops | bytes accessed | tf_op | source)
XLA Modules:
  0.0 83.4 jit_solution(14556150421535060238)
XLA Ops:
  0.6 81.3 %gradient_step.1 = (bf16[192,128]{1,0:T(8,128)(2,1)}, f32[4,1024]{1,0:T(4,128)}, f32[4,64]{1,0:T(4,128)}) custom-call(bf16[192,1024]{1,0:T(8,128)(2,1)} %inputs_hbm.1, bf16[1024,1024]{1,0:T(8,128)(2,1)} %w_first_hbm.1, bf16[64,1024]{1,0:T(8,128)(2,1)} %bitcast.2, f32[1,64]{1,0:T(1,128)} %bitcast.3, bf16[192,128]{1,0:T(8,128)(2,1)} %probes_hbm.1, ...), custom_call_target="tpu_custom_call" | custom-call | tf_op jit(solution)/shard_map/gradient_step/pallas_call | solution.py:623
  82.0 1.4 %settle.1 = (bf16[192,128]{1,0:T(8,128)(2,1)}, f32[4,1024]{1,0:T(4,128)}, f32[4,64]{1,0:T(4,128)}) custom-call(bf16[192,128]{1,0:T(8,128)(2,1)} %get-tuple-element.6.products, f32[4,1024]{1,0:T(4,128)} %get-tuple-element.7.grad_first, f32[4,64]{1,0:T(4,128)} %get-tuple-element.8.grad_second), custom_call_target="tpu_custom_call" | custom-call | tf_op jit(solution)/shard_map/settle/pallas_call | solution.py:668

commit v3 on v2

--- a/solution.py
+++ b/solution.py
@@ -85,10 +85,10 @@
     inputs_hbm, w_first_hbm, w_second_hbm, inv_length, probes_hbm, solves_hbm,
     products, grad_first, grad_second,
     w_first, w_second, row_p, row_s, row_u, col_p, col_s, col_u, cross_t, inner_t, mix,
-    left_near, near_v, near_m, near_s, out_v, out_d, got_v, got_d,
+    left_near, left_next, near_v, near_m, near_s, out_v, out_d, got_v, got_d,
     group_x, group_xt, factor, hidden_t, group_d,
     chunks, got_chunks, pieces, got_pieces,
-    load_sem, row_send, row_recv, up_send, down_send, side_send, col_recv,
+    load_sem, weight_sem, row_send, row_recv, up_send, down_send, side_send, col_recv,
     out_send, out_recv, x_send, x_recv, d_send, d_recv,
     chunk_send, chunk_recv, piece_send, piece_recv,
 ):
@@ -126,34 +126,44 @@
 
     barrier = pltpu.get_barrier_semaphore()
 
-    def greet_plane(step, carry):
-        px, py = plane_peer(step, 1)
-        pl.semaphore_signal(barrier, inc=1, device_id=device(px, py, z, core), device_id_type=MESH)
-        return carry
-
-    def greet_column(step, carry):
-        pz, pc = column_peer(step)
-        pl.semaphore_signal(barrier, inc=1, device_id=device(x, y, pz, pc), device_id_type=MESH)
-        return carry
-
-    lax.fori_loop(1, PLANE, greet_plane, 0)
-    lax.fori_loop(1, COLS, greet_column, 0)
-
     loads = [
         pltpu.make_async_copy(source, target, load_sem.at[index])
         for index, (source, target) in enumerate((
-            (inputs_hbm, group_x.at[member]), (w_first_hbm, w_first), (w_second_hbm, w_second),
+            (inputs_hbm, group_x.at[member]), (w_second_hbm, w_second),
             (probes_hbm, col_p.at[OWN]), (solves_hbm, col_s.at[OWN]),
             (probes_hbm, row_p.at[0]), (solves_hbm, row_s.at[0]),
         ))
     ]
-    for load in loads:
+
+    def load_weights(block):
+        here = pl.ds(pl.multiple_of(block * 256, 256), 256)
+        return pltpu.make_async_copy(w_first_hbm.at[:, here], w_first.at[:, here], weight_sem.at[block])
+
+    loads[0].start()
+    for block in range(HID // 256):
+        load_weights(block).start()
+    for load in loads[1:]:
         load.start()
-    for load in loads:
-        load.wait()
+
+    def greet_plane(step, carry):
+        px, py = plane_peer(step, 1)
+        pl.semaphore_signal(barrier, inc=1, device_id=device(px, py, z, core), device_id_type=MESH)
+        return carry
+
+    def greet_column(step, carry):
+        pz, pc = column_peer(step)
+        pl.semaphore_signal(barrier, inc=1, device_id=device(x, y, pz, pc), device_id_type=MESH)
+        return carry
+
+    lax.fori_loop(1, PLANE, greet_plane, 0)
+    lax.fori_loop(1, COLS, greet_column, 0)
+
+    loads[0].wait()
+    loads[1].wait()
 
     def encode(block, total):
         start = pl.multiple_of(block * 256, 256)
+        load_weights(block).wait()
         pre = dot(group_x[member], w_first[:, pl.ds(start, 256)])
         hidden = (pre * jax.nn.sigmoid(pre)).astype(bf16)
         hidden_t[pl.ds(start, 256), :] = hidden.T
@@ -164,6 +174,9 @@
     packed = pack_rows(scaled)
     col_u[OWN] = packed
     row_u[0] = packed
+
+    for load in loads[2:]:
+        load.wait()
 
     pl.semaphore_wait(barrier, 30)
 
@@ -248,8 +261,8 @@
         row_wait(which, STEPS.index(block))
         spread(which, block)
 
-    def wave(level):
-        for which in range(3):
+    def wave(level, items=(0, 1, 2)):
+        for which in items:
             for block in STEPS[1:]:
                 first, turn = ways[which]
                 far = [0 if item == 0 else 2 if item == 2 else 1 for item in block]
@@ -263,8 +276,8 @@
         spread(which, (0, 0))
         side_copy(which, OWN, OWN + 1).start()
 
-    def advance(far):
-        for which in range(3):
+    def advance(far, items=(0, 1, 2)):
+        for which in items:
             here = up_slot(far)
             column_wait(which, here)
 
@@ -303,18 +316,19 @@
     near_v[...] = jnp.zeros_like(near_v)
     near_m[...] = jnp.zeros_like(near_m)
     near_s[...] = jnp.zeros_like(near_s)
-    wave(1)
-    advance(1)
-    for block in STEPS[1:NEAR]:
-        for which in range(3):
-            if (which, block) not in waited:
-                take(which, block)
-
     def near_row(step, carry):
         left_near[pl.ds(pl.multiple_of(step * ROWS, ROWS), ROWS), :] = row_operand(step)[0]
         return carry
 
-    lax.fori_loop(0, NEAR, near_row, 0)
+    for items in ((0,), (1, 2)):
+        advance(1, items)
+        wave(1, items)
+        for block in STEPS[1:NEAR]:
+            for which in items:
+                if (which, block) not in waited:
+                    take(which, block)
+        if 0 in items:
+            lax.fori_loop(0, NEAR, near_row, 0)
 
     def prepare(pair):
         slot = 2 * pair
@@ -449,7 +463,9 @@
 
     def row_block(index, carry):
         step = PLANE - 1 - index
-        left, wide = row_operand(step)
+        wide = unpack_rows(row_u[step]).astype(f32)
+        left = left_next[lax.rem(index, 2)]
+        left_next[lax.rem(index + 1, 2)] = row_operand(jnp.maximum(step - 1, NEAR))[0]
         inner = jnp.concatenate([row_s[step], row_p[step]], axis=1)
         total = None
         block = 1024
@@ -460,6 +476,7 @@
         finish_rows(step, *total, wide)
         return carry
 
+    left_next[0] = row_operand(PLANE - 1)[0]
     lax.fori_loop(0, PLANE - EARLY, row_block, 0)
 
     for step in range(1, GROUP):
@@ -492,12 +509,31 @@
     for step in range(1, GROUP):
         group_copy(step, group_d.at[member], group_d, d_send, d_recv).start()
 
+    def place(px, py):
+        return 2 * (4 * lax.rem(px, 2) + py) + lax.div(px, 2)
+
+    def chunk_copy(step, part):
+        px, py = plane_peer(step, 1)
+        here = (pl.ds(0, 64 * LANES), pl.ds(64 * LANES, 32))[part]
+        return remote(
+            chunks.at[place(px, py), here], got_chunks.at[step, here],
+            chunk_send.at[part, step], chunk_recv.at[part, step], device(px, py, z, core),
+        )
+
+    def send_chunk(part):
+        def send(step, carry):
+            chunk_copy(step, part).start()
+            return carry
+
+        return send
+
     second = dot(hidden_t[...], unpack_rows(packed_d))
     low = jnp.concatenate([second[: HID // 2], second[HID // 2:]], axis=1).astype(bf16)
     for far in range(4):
         tile = 8 * LANES + far
         chunks[:, tile * 8:tile * 8 + 8, :] = low[128 * far:128 * far + 128].reshape(PLANE, 8, 128)
 
+    lax.fori_loop(1, PLANE, send_chunk(1), 0)
     for step in range(1, GROUP):
         group_wait(step, group_d.at[member], group_d, d_send, d_recv)
     whole_d = jnp.concatenate([unpack_rows(group_d[item]) for item in range(GROUP)], axis=0)
@@ -509,24 +545,11 @@
             tile = far * LANES + lane
             chunks[:, tile * 8:tile * 8 + 8, :] = first[:, 128 * lane:128 * lane + 128].reshape(PLANE, 8, 128)
 
-    def place(px, py):
-        return 2 * (4 * lax.rem(px, 2) + py) + lax.div(px, 2)
-
-    def chunk_copy(step):
-        px, py = plane_peer(step, 1)
-        return remote(
-            chunks.at[place(px, py)], got_chunks.at[step], chunk_send.at[step], chunk_recv.at[step],
-            device(px, py, z, core),
-        )
-
-    def send_chunk(step, carry):
-        chunk_copy(step).start()
-        return carry
-
-    lax.fori_loop(1, PLANE, send_chunk, 0)
+    lax.fori_loop(1, PLANE, send_chunk(0), 0)
 
     def add_chunk(step, total):
-        chunk_copy(step).wait_recv()
+        chunk_copy(step, 1).wait_recv()
+        chunk_copy(step, 0).wait_recv()
         return total + got_chunks[step].astype(f32)
 
     summed = lax.fori_loop(1, PLANE, add_chunk, chunks[place(x, y)].astype(f32))
@@ -590,7 +613,8 @@
             ).wait_send()
         for which in range(2):
             out_copy(step, which).wait_send()
-        chunk_copy(step).wait_send()
+        chunk_copy(step, 0).wait_send()
+        chunk_copy(step, 1).wait_send()
         return carry
 
     lax.fori_loop(1, PLANE, finish_plane, 0)
@@ -638,6 +662,7 @@
             pltpu.VMEM((2 * PROBES, WIDTH), bf16),
             pltpu.VMEM((WIDTH, FEAT), bf16),
             pltpu.VMEM((EARLY * ROWS, 4 * FEAT), bf16),
+            pltpu.VMEM((2, ROWS, 4 * FEAT), bf16),
             pltpu.VMEM((EARLY * ROWS, PROBES), f32),
             pltpu.VMEM((EARLY * ROWS, FEAT), f32),
             pltpu.VMEM((EARLY * ROWS, 128), f32),
@@ -654,11 +679,11 @@
             pltpu.VMEM((PLANE, TILES * 8, 128), bf16),
             pltpu.VMEM((8, 8 * LANES + 8, 128), bf16),
             pltpu.VMEM((COLS, 8 * LANES + 8, 128), bf16),
-            dma((7,)), dma((3, PLANE)), dma((3, PLANE)),
+            dma((6,)), dma((HID // 256,)), dma((3, PLANE)), dma((3, PLANE)),
             dma((3, 4)), dma((3, 4)), dma((3, COLS)), dma((3, COLS)),
             dma((2, PLANE)), dma((2, PLANE)),
             dma((GROUP,)), dma((GROUP,)), dma((GROUP,)), dma((GROUP,)),
-            dma((PLANE,)), dma((PLANE,)), dma((COLS,)), dma((COLS,)),
+            dma((2, PLANE)), dma((2, PLANE)), dma((COLS,)), dma((COLS,)),
         ],
         compiler_params=pltpu.CompilerParams(
             collective_id=0, has_side_effects=True, vmem_limit_bytes=56 * 1024 * 1024

time: 83.6 us -> 80.2 us (0.959)
  Pallas kernels: 82.8 us -> 79.4 us
    pallas_call x1, Pallas kernels: 81.3 us -> 77.9 us  [local(): pl.pallas_call(kernel, out_shape=shapes, in_specs=[hbm, hbm, hbm, vmem, h...]
where the time goes in v3:
time: 80.2 us; the launch traced here: 80 us
  Pallas kernels  79.4 us (99%)
    pallas_call x1, Pallas kernels, local(): pl.pallas_call(kernel, out_shape=shapes, in_specs=[hbm, hbm, hbm, vmem, h...  77.9 us

profile of v3, /device:TPU:1, one launch (start us, length us, event | category | flops | bytes accessed | tf_op | source)
XLA Modules:
  0.0 80.0 jit_solution(5157854442178042080)
XLA Ops:
  0.6 77.9 %gradient_step.1 = (bf16[192,128]{1,0:T(8,128)(2,1)}, f32[4,1024]{1,0:T(4,128)}, f32[4,64]{1,0:T(4,128)}) custom-call(bf16[192,1024]{1,0:T(8,128)(2,1)} %inputs_hbm.1, bf16[1024,1024]{1,0:T(8,128)(2,1)} %w_first_hbm.1, bf16[64,1024]{1,0:T(8,128)(2,1)} %bitcast.2, f32[1,64]{1,0:T(1,128)} %bitcast.3, bf16[192,128]{1,0:T(8,128)(2,1)} %probes_hbm.1, ...), custom_call_target="tpu_custom_call" | custom-call | tf_op jit(solution)/shard_map/gradient_step/pallas_call | solution.py:647
  78.6 1.4 %settle.1 = (bf16[192,128]{1,0:T(8,128)(2,1)}, f32[4,1024]{1,0:T(4,128)}, f32[4,64]{1,0:T(4,128)}) custom-call(bf16[192,128]{1,0:T(8,128)(2,1)} %get-tuple-element.6.products, f32[4,1024]{1,0:T(4,128)} %get-tuple-element.7.grad_first, f32[4,64]{1,0:T(4,128)} %get-tuple-element.8.grad_second), custom_call_target="tpu_custom_call" | custom-call | tf_op jit(solution)/shard_map/settle/pallas_call | solution.py:693

commit v4 on v3

--- a/solution.py
+++ b/solution.py
@@ -43,7 +43,7 @@
 )
 PAIR = 2 * ROWS
 CHUNK = 4 * ROWS
-OWN = 12
+OWN = 2
 
 
 def dot_nt(left, right):
@@ -185,8 +185,8 @@
 
     def up_slot(far):
         if isinstance(far, int):
-            return (OWN, 0, 4, 8, OWN + 2)[far]
-        return jnp.where(far == 4, OWN + 2, 4 * far - 4)
+            return (OWN, 0, 4, 8, 12)[far]
+        return 4 * far - 4
 
     def down_slot(far):
         if isinstance(far, int):
@@ -285,7 +285,7 @@
             def _():
                 up_copy(which, far).start()
 
-            side_copy(which, here, jnp.where(far == 4, OWN + 3, 4 * far - 2)).start()
+            side_copy(which, here, jnp.where(far == 4, 13, 4 * far + 2)).start()
 
             @pl.when(far < 4)
             def _():
@@ -295,7 +295,7 @@
                 def _():
                     down_copy(which, far).start()
 
-                side_copy(which, down_slot(far), 4 * far - 1).start()
+                side_copy(which, down_slot(far), 4 * far + 3).start()
 
     def group_copy(step, source, buffer, send, recv):
         other = lax.rem(member + step, GROUP)
@@ -406,15 +406,18 @@
         @pl.when(far <= 4)
         def _():
             for which in range(3):
-                @pl.when(far < 4)
+                @pl.when(far == 1)
+                def _():
+                    column_wait(which, OWN + 1)
+
+                @pl.when(far > 1)
                 def _():
                     column_wait(which, 4 * far - 2)
                     column_wait(which, 4 * far - 1)
 
                 @pl.when(far == 4)
                 def _():
-                    column_wait(which, OWN + 1)
-                    column_wait(which, OWN + 3)
+                    column_wait(which, 13)
 
             prepare(2 * far - 2)
             prepare(2 * far - 1)
@@ -602,8 +605,8 @@
             up_copy(which, far).wait_send()
         for far in range(3):
             down_copy(which, far).wait_send()
-        for slot in (0, 1, 4, 5, 8, 9, OWN, OWN + 2):
-            side_copy(which, slot, 2).wait_send()
+        for slot in (0, 1, 4, 5, 8, 9, 12, OWN):
+            side_copy(which, slot, 3).wait_send()
 
     def finish_plane(step, carry):
         for which in range(3):

time: 80.2 us -> 79.2 us (0.988)
  Pallas kernels: 79.4 us -> 78.4 us
    pallas_call x1, Pallas kernels: 77.9 us -> 76.9 us  [local(): pl.pallas_call(kernel, out_shape=shapes, in_specs=[hbm, hbm, hbm, vmem, h...]
where the time goes in v4:
time: 79.2 us; the launch traced here: 79 us
  Pallas kernels  78.4 us (99%)
    pallas_call x1, Pallas kernels, local(): pl.pallas_call(kernel, out_shape=shapes, in_specs=[hbm, hbm, hbm, vmem, h...  76.9 us

profile of v4, /device:TPU:1, one launch (start us, length us, event | category | flops | bytes accessed | tf_op | source)
XLA Modules:
  0.0 79.0 jit_solution(6050031975261911361)
XLA Ops:
  0.6 76.9 %gradient_step.1 = (bf16[192,128]{1,0:T(8,128)(2,1)}, f32[4,1024]{1,0:T(4,128)}, f32[4,64]{1,0:T(4,128)}) custom-call(bf16[192,1024]{1,0:T(8,128)(2,1)} %inputs_hbm.1, bf16[1024,1024]{1,0:T(8,128)(2,1)} %w_first_hbm.1, bf16[64,1024]{1,0:T(8,128)(2,1)} %bitcast.2, f32[1,64]{1,0:T(1,128)} %bitcast.3, bf16[192,128]{1,0:T(8,128)(2,1)} %probes_hbm.1, ...), custom_call_target="tpu_custom_call" | custom-call | tf_op jit(solution)/shard_map/gradient_step/pallas_call | solution.py:650
  77.5 1.4 %settle.1 = (bf16[192,128]{1,0:T(8,128)(2,1)}, f32[4,1024]{1,0:T(4,128)}, f32[4,64]{1,0:T(4,128)}) custom-call(bf16[192,128]{1,0:T(8,128)(2,1)} %get-tuple-element.6.products, f32[4,1024]{1,0:T(4,128)} %get-tuple-element.7.grad_first, f32[4,64]{1,0:T(4,128)} %get-tuple-element.8.grad_second), custom_call_target="tpu_custom_call" | custom-call | tf_op jit(solution)/shard_map/settle/pallas_call | solution.py:696

commit v5 on v4

--- a/solution.py
+++ b/solution.py
@@ -410,17 +410,16 @@
                 def _():
                     column_wait(which, OWN + 1)
 
-                @pl.when(far > 1)
-                def _():
-                    column_wait(which, 4 * far - 2)
-                    column_wait(which, 4 * far - 1)
-
                 @pl.when(far == 4)
                 def _():
                     column_wait(which, 13)
 
             prepare(2 * far - 2)
-            prepare(2 * far - 1)
+
+            @pl.when(far == 1)
+            def _():
+                prepare(1)
+
             near_tile(0, NEAR, far - 1)
 
         @pl.when(far == 4)
@@ -429,6 +428,10 @@
 
         @pl.when(far < 4)
         def _():
+            for which in range(3):
+                column_wait(which, 4 * far + 2)
+                column_wait(which, 4 * far + 3)
+            prepare(2 * far + 1)
             advance(far + 1)
 
         @pl.when(far == 1)

time: 79.2 us -> 78.8 us (level)
  no operation moved by 1% of the time
where the time goes in v5:
time: 78.8 us; the launch traced here: 78.6 us
  Pallas kernels  78 us (99%)
    pallas_call x1, Pallas kernels, local(): pl.pallas_call(kernel, out_shape=shapes, in_specs=[hbm, hbm, hbm, vmem, h...  76.6 us

profile of v5, /device:TPU:1, one launch (start us, length us, event | category | flops | bytes accessed | tf_op | source)
XLA Modules:
  0.0 78.6 jit_solution(9762116452578423919)
XLA Ops:
  0.6 76.6 %gradient_step.1 = (bf16[192,128]{1,0:T(8,128)(2,1)}, f32[4,1024]{1,0:T(4,128)}, f32[4,64]{1,0:T(4,128)}) custom-call(bf16[192,1024]{1,0:T(8,128)(2,1)} %inputs_hbm.1, bf16[1024,1024]{1,0:T(8,128)(2,1)} %w_first_hbm.1, bf16[64,1024]{1,0:T(8,128)(2,1)} %bitcast.2, f32[1,64]{1,0:T(1,128)} %bitcast.3, bf16[192,128]{1,0:T(8,128)(2,1)} %probes_hbm.1, ...), custom_call_target="tpu_custom_call" | custom-call | tf_op jit(solution)/shard_map/gradient_step/pallas_call | solution.py:653
  77.2 1.4 %settle.1 = (bf16[192,128]{1,0:T(8,128)(2,1)}, f32[4,1024]{1,0:T(4,128)}, f32[4,64]{1,0:T(4,128)}) custom-call(bf16[192,128]{1,0:T(8,128)(2,1)} %get-tuple-element.6.products, f32[4,1024]{1,0:T(4,128)} %get-tuple-element.7.grad_first, f32[4,64]{1,0:T(4,128)} %get-tuple-element.8.grad_second), custom_call_target="tpu_custom_call" | custom-call | tf_op jit(solution)/shard_map/settle/pallas_call | solution.py:699
